TPU v7x, 32 devices: a whole 2x2x4 slice. The times are simulated.
32 devices in a mesh: replica: 2 (over core), shard: 16 (over z, y, x).
Axes of the slice: x: 2, y: 2, z: 4, core: 2. Of those that a mesh axis runs over, the one named last changes fastest.
Arguments:
- gradients: bfloat16 [2, 2, 16, 1024, 256], P('replica', None, None, 'shard'), may hold values from -36 to 36
- momentum: float32 [2, 16, 1024, 256], P('replica', None, 'shard'), may hold values from -3 to 3
- params: float32 [16, 1024, 256], P(None, ('shard', 'replica')), may hold values from -6 to 6
- outer_moment: float32 [16, 1024, 256], P(None, ('shard', 'replica')), may hold values from -2 to 2
- shadow: float32 [16, 1024, 256], P(None, ('shard', 'replica')), may hold values from -6 to 6
Outputs:
- new_params: float32 [16, 1024, 256], P(None, ('shard', 'replica'))
- new_outer_moment: float32 [16, 1024, 256], P(None, ('shard', 'replica'))
- new_shadow: float32 [16, 1024, 256], P(None, ('shard', 'replica'))
- new_momentum: float32 [2, 16, 1024, 256], P('replica', None, 'shard')
All inputs are finite; a program needn't handle non-finite values.
Results may differ from a plain program's by a relative error of at most 0.0085.
Values may be sent and summed in bfloat16 or wider, within the bound.
No kernel may reach another device: no remote copies, remote signals or barrier semaphores. Data moves between devices by JAX's collectives and lax.ppermute only.
A program may use at most 64 MiB of HBM per device.

v0:
```python
import math
import jax
import jax.numpy as jnp
from jax import lax
from jax.sharding import PartitionSpec as P

NS_ITERS = 5
quintic_a = 3.4445
quintic_b = -4.775
quintic_c = 2.0315
inner_beta = 0.95
outer_mu = 0.9
outer_rate = 0.7
shadow_decay = 0.9


def newton_schulz(block):
    squares = jnp.sum(jnp.square(block.astype(jnp.float32)))
    current = (block.astype(jnp.float32) / (jnp.sqrt(squares) + 1e-07)).astype(jnp.bfloat16)
    for _ in range(NS_ITERS):
        gram = jnp.einsum("di,dj->ij", current, current, preferred_element_type=jnp.float32).astype(
            jnp.bfloat16
        )
        square = jnp.dot(gram, gram, preferred_element_type=jnp.float32)
        poly = (quintic_b * gram.astype(jnp.float32) + quintic_c * square).astype(jnp.bfloat16)
        product = jnp.dot(current, poly, preferred_element_type=jnp.float32)
        current = (quintic_a * current.astype(jnp.float32) + product).astype(jnp.bfloat16)
    return current


def body(gradients, momentum, params, outer_moment, shadow):
    shards = lax.axis_size("shard")
    replicas = lax.axis_size("replica")
    _, inner, mats, rows, width = gradients.shape
    owned = mats // shards
    total_rows = rows * shards
    rows_each = rows // replicas
    scale_step = 0.2 * math.sqrt(total_rows)
    moment = momentum[0]
    updates = []
    for k in range(inner):
        grad = gradients[0, k].astype(jnp.float32)
        moment = inner_beta * moment + grad
        updates.append((grad + inner_beta * moment).astype(jnp.bfloat16))
    stacked = jnp.stack(updates, axis=1)
    moved = lax.all_to_all(stacked, "shard", split_axis=0, concat_axis=0, tiled=True)
    moved = moved.reshape((shards, owned, inner, rows, width))
    totals = []
    for m in range(owned):
        total = None
        for k in range(inner):
            ortho = newton_schulz(moved[:, m, k].reshape((total_rows, width)))
            term = scale_step * ortho.astype(jnp.float32)
            total = term if total is None else total + term
        totals.append(total)
    total = jnp.stack(totals).reshape((owned, shards, replicas, rows_each, width))
    me = lax.axis_index("replica")
    summed = lax.dynamic_index_in_dim(total, me, 2, keepdims=False)
    for step in range(1, replicas):
        theirs = lax.dynamic_index_in_dim(total, (me + step) % replicas, 2, keepdims=False)
        got = lax.ppermute(
            theirs.astype(jnp.bfloat16),
            "replica",
            [(i, (i + step) % replicas) for i in range(replicas)],
        )
        summed = summed + got.astype(jnp.float32)
    placed = lax.all_to_all(
        summed.astype(jnp.bfloat16), "shard", split_axis=1, concat_axis=0, tiled=True
    )
    outer_delta = placed.reshape((mats, rows_each, width)).astype(jnp.float32) / replicas
    new_outer = outer_mu * outer_moment + outer_delta
    new_params = params - outer_rate * (outer_delta + outer_mu * new_outer)
    new_shadow = shadow_decay * shadow + (1.0 - shadow_decay) * new_params
    return (new_params, new_outer, new_shadow, moment[None])


def solution(mesh):
    rows = P(None, ("shard", "replica"), None)
    mine = P("replica", None, "shard", None)
    return jax.shard_map(
        body,
        mesh=mesh,
        in_specs=(P("replica", None, None, "shard", None), mine, rows, rows, rows),
        out_specs=(rows, rows, rows, mine),
        check_vma=False,
    )
```

profile of v0, /device:TPU:0, one launch (start us, length us, event | category | flops | bytes accessed | tf_op | source)
XLA Modules:
  0.0 83.9 jit_solution(12345464679178923116)
XLA Ops:
  0.7 2.0 %fusion.51 = bf16[16,1,64,256]{3,2,1,0:T(8,128)(2,1)S(1)} fusion(f32[1,16,64,256]{3,2,1,0:T(8,128)} %param.6, bf16[1,2,16,64,256]{4,3,2,1,0:T(8,128)(2,1)} %param.5), kind=kLoop, calls=%fused_computation.89 | loop fusion | flops 2359296 | bytes 2621440 | tf_op jit(solution)/shard_map/convert_element_type | solution.py:44
  3.0 1.1 %pad_maximum_fusion = bf16[16,2,64,256]{3,2,1,0:T(8,128)(2,1)} fusion(bf16[16,1,64,256]{3,2,1,0:T(8,128)(2,1)S(1)} %fusion.51, bf16[16,1,64,256]{3,2,1,0:T(8,128)(2,1)S(1)} %fusion.52), kind=kLoop, calls=%fused_computation.90 | loop fusion | flops 524288 | bytes 2097152 | tf_op jit(solution)/shard_map/stack | solution.py:45
  4.1 8.4 %all-to-all-start = ((bf16[16,2,64,256]{3,2,1,0:T(8,128)(2,1)}), bf16[16,2,64,256]{3,2,1,0:T(8,128)(2,1)}, u32[]{:S(2)}, u32[]{:S(2)}) async-start(bf16[16,2,64,256]{3,2,1,0:T(8,128)(2,1)} %pad_maximum_fusion), calls=%async_computation | async-start | bytes 2097152 | tf_op jit(solution)/shard_map/all_to_all | solution.py:46
  12.5 24.4 %all-to-all-done = bf16[16,2,64,256]{3,2,1,0:T(8,128)(2,1)} async-done(((bf16[16,2,64,256]{3,2,1,0:T(8,128)(2,1)}), bf16[16,2,64,256]{3,2,1,0:T(8,128)(2,1)}, u32[]{:S(2)}, u32[]{:S(2)}) %all-to-all-start) | async-done | bytes 1048608 | tf_op jit(solution)/shard_map/all_to_all | solution.py:46
  36.9 1.3 %copy.17 = bf16[16,2,64,256]{3,2,0,1:T(8,128)(2,1)S(1)} copy(bf16[16,2,64,256]{3,2,1,0:T(8,128)(2,1)} %all-to-all-done) | data formatting | bytes 2097152 | tf_op jit(solution)/shard_map/all_to_all | solution.py:46
  38.2 0.9 %fusion.40 = (f32[]{:T(128)}, f32[]{:T(128)}) fusion(bf16[16,1,2,64,256]{4,3,0,2,1:T(8,128)(2,1)S(1)} %bitcast.151), kind=kLoop, calls=%fused_computation.78 | loop fusion | flops 1572862 | bytes 1048584 | tf_op jit(solution)/shard_map/reduce_sum | solution.py:18
  40.5 1.0 %fusion.41 = (bf16[16,1,1,64,256]{4,3,0,2,1:T(8,128)(2,1)S(1)}, bf16[16,1,1,64,256]{4,3,0,2,1:T(8,128)(2,1)}) fusion(f32[]{:T(128)S(6)} %add.149, bf16[16,1,2,64,256]{4,3,0,2,1:T(8,128)(2,1)S(1)} %bitcast.152, f32[]{:T(128)S(6)} %add.160), kind=kLoop, calls=%fused_computation.79 | loop fusion | flops 1572864 | bytes 2097160 | tf_op jit(solution)/shard_map/convert_element_type | solution.py:19
  41.9 0.4 copy-done.7
  42.3 1.7 %fusion.4 = bf16[1024,256]{1,0:T(8,128)(2,1)S(1)} fusion(bf16[1024,256]{1,0:T(8,128)(2,1)} %bitcast.156, bf16[256,256]{1,0:T(8,128)(2,1)S(1)} %fusion.28), kind=kOutput, calls=%fused_computation.22 | convolution fusion | flops 169148416 | bytes 1179648 | tf_op jit(solution)/shard_map/dot_general | solution.py:26
  44.0 0.3 convolution_convert_fusion.7
  44.4 0.5 fusion.5
  44.9 0.3 convolution_convert_fusion.6
  45.3 0.5 fusion.6
  45.8 0.8 copy-done.8
  46.9 1.7 %fusion.7 = bf16[1024,256]{1,0:T(8,128)(2,1)S(1)} fusion(bf16[1024,256]{1,0:T(8,128)(2,1)} %copy-done.8, bf16[256,256]{1,0:T(8,128)(2,1)S(1)} %convolution_convert_fusion.5), kind=kOutput, calls=%fused_computation.25 | convolution fusion | flops 169148416 | bytes 1179648 | tf_op jit(solution)/shard_map/dot_general | solution.py:26
  49.0 0.4 copy-done.5
  49.5 0.4 copy-done.6
  50.3 0.5 fusion.12
  51.1 0.5 fusion.13
  52.0 0.5 fusion.14
  52.6 0.8 copy-done.9
  53.7 1.7 %fusion.15 = bf16[1024,256]{1,0:T(8,128)(2,1)S(1)} fusion(bf16[1024,256]{1,0:T(8,128)(2,1)} %copy-done.9, bf16[256,256]{1,0:T(8,128)(2,1)S(1)} %convolution_convert_fusion.1), kind=kOutput, calls=%fused_computation.33 | convolution fusion | flops 169148416 | bytes 1179648 | tf_op jit(solution)/shard_map/dot_general | solution.py:26
  55.4 0.8 copy-done.2
  56.6 1.7 %fusion.17 = f32[1024,256]{1,0:T(8,128)S(1)} fusion(bf16[1024,256]{1,0:T(8,128)(2,1)} %copy-done.2, bf16[256,256]{1,0:T(8,128)(2,1)S(1)} %convolution_convert_fusion), kind=kOutput, calls=%fused_computation.35 | convolution fusion | flops 169410560 | bytes 1703936 | tf_op jit(solution)/shard_map/dot_general | solution.py:26
  58.3 2.7 %fusion.11 = f32[1024,256]{1,0:T(8,128)} fusion(f32[1024,256]{1,0:T(8,128)S(1)} %fusion.17, bf16[1024,256]{1,0:T(8,128)(2,1)} %copy-done.5, bf16[256,256]{1,0:T(8,128)(2,1)S(1)} %convolution_convert_fusion.4), kind=kOutput, calls=%fused_computation.29 | convolution fusion | flops 169934848 | bytes 2752512 | tf_op jit(solution)/shard_map/dot_general | solution.py:26
  61.0 1.1 %fusion.58 = bf16[1,16,32,256]{3,2,0,1:T(8,128)(2,1)S(1)} fusion(f32[1,16,2,32,256]{4,3,2,1,0:T(8,128)} %bitcast.153, s32[]{:T(128)S(6)} %select_n.16), kind=kLoop, calls=%fused_computation.104 | loop fusion | bytes 524292 | tf_op jit(solution)/shard_map/convert_element_type | solution.py:62
  62.1 1.5 %collective-permute-done = bf16[1,16,32,256]{3,2,0,1:T(8,128)(2,1)S(1)} collective-permute-done((bf16[1,16,32,256]{3,2,0,1:T(8,128)(2,1)S(1)}, bf16[1,16,32,256]{3,2,0,1:T(8,128)(2,1)S(1)}, u32[]{:S(2)}, u32[]{:S(2)}) %collective-permute-start) | collective-permute-done | bytes 262176 | tf_op jit(solution)/shard_map/ppermute | solution.py:61
  63.7 1.8 %fusion.55 = bf16[1,16,32,256]{3,2,0,1:T(8,128)(2,1)} fusion(bf16[1,16,32,256]{3,2,0,1:T(8,128)(2,1)S(1)} %collective-permute-done, f32[1,16,2,32,256]{4,3,2,1,0:T(8,128)} %bitcast.154, s32[]{:T(128)S(6)} %select_n.14), kind=kLoop, calls=%fused_computation.99 | loop fusion | flops 393216 | bytes 1048580 | tf_op jit(solution)/shard_map/convert_element_type | solution.py:68
  65.5 5.9 %all-to-all-start.1 = ((bf16[1,16,32,256]{3,2,0,1:T(8,128)(2,1)}), bf16[1,16,32,256]{3,2,0,1:T(8,128)(2,1)S(1)}, u32[]{:S(2)}, u32[]{:S(2)}) async-start(bf16[1,16,32,256]{3,2,0,1:T(8,128)(2,1)} %fusion.55), calls=%async_computation.1 | async-start | bytes 524288 | tf_op jit(solution)/shard_map/all_to_all | solution.py:67
  71.4 1.2 %fusion.49 = f32[1,16,64,256]{3,2,1,0:T(8,128)} fusion(f32[1,16,64,256]{3,2,1,0:T(8,128)S(1)} %copy-done, bf16[1,2,16,64,256]{4,3,2,1,0:T(8,128)(2,1)S(1)} %copy-done.1), kind=kLoop, calls=%fused_computation.87 | loop fusion | flops 1572864 | bytes 3145728 | tf_op jit(solution)/shard_map/add | solution.py:43
  72.6 8.9 %all-to-all-done.1 = bf16[1,16,32,256]{3,2,0,1:T(8,128)(2,1)S(1)} async-done(((bf16[1,16,32,256]{3,2,0,1:T(8,128)(2,1)}), bf16[1,16,32,256]{3,2,0,1:T(8,128)(2,1)S(1)}, u32[]{:S(2)}, u32[]{:S(2)}) %all-to-all-start.1) | async-done | bytes 262176 | tf_op jit(solution)/shard_map/all_to_all | solution.py:67
  81.5 2.4 %multiply_add_fusion = (f32[16,32,256]{2,1,0:T(8,128)}, f32[16,32,256]{2,1,0:T(8,128)}, f32[16,32,256]{2,1,0:T(8,128)}) fusion(f32[16,32,256]{2,1,0:T(8,128)S(1)} %copy-done.3, f32[16,32,256]{2,1,0:T(8,128)S(1)} %copy-done.4, bf16[1,16,32,256]{3,2,0,1:T(8,128)(2,1)S(1)} %all-to-all-done.1, f32[16,32,256]{2,1,0:T(8,128)} %param.8), kind=kLoop, calls=%fused_computation.102 | loop fusion | flops 1441792 | bytes 3407872 | tf_op jit(solution)/shard_map/add | solution.py:73
  (24 shorter events, 3.2 us)
Async XLA Ops:
  0.6 2.0 %copy-start.1 = (bf16[1,2,16,64,256]{4,3,2,1,0:T(8,128)(2,1)S(1)}, bf16[1,2,16,64,256]{4,3,2,1,0:T(8,128)(2,1)}, u32[]{:S(2)}) copy-start(bf16[1,2,16,64,256]{4,3,2,1,0:T(8,128)(2,1)} %param.5) | copy-start | bytes 3145732
  0.6 2.2 %copy-start = (f32[1,16,64,256]{3,2,1,0:T(8,128)S(1)}, f32[1,16,64,256]{3,2,1,0:T(8,128)}, u32[]{:S(2)}) copy-start(f32[1,16,64,256]{3,2,1,0:T(8,128)} %param.6) | copy-start | bytes 3145732
  4.1 32.8 %all-to-all-start = ((bf16[16,2,64,256]{3,2,1,0:T(8,128)(2,1)}), bf16[16,2,64,256]{3,2,1,0:T(8,128)(2,1)}, u32[]{:S(2)}, u32[]{:S(2)}) async-start(bf16[16,2,64,256]{3,2,1,0:T(8,128)(2,1)} %pad_maximum_fusion), calls=%async_computation | async-start | bytes 2097152 | tf_op jit(solution)/shard_map/all_to_all | solution.py:46
  41.5 0.8 copy-start.7
  45.8 0.8 copy-start.8
  48.7 0.8 copy-start.5
  48.7 1.2 %copy-start.6 = (bf16[16,1,1,64,256]{4,3,0,2,1:T(8,128)(2,1)S(1)}, bf16[16,1,1,64,256]{4,3,0,2,1:T(8,128)(2,1)}, u32[]{:S(2)}) copy-start(bf16[16,1,1,64,256]{4,3,0,2,1:T(8,128)(2,1)} %get-tuple-element.10) | copy-start | bytes 1572868
  52.5 0.8 copy-start.9
  55.4 0.8 copy-start.2
  62.1 1.6 %collective-permute-start = (bf16[1,16,32,256]{3,2,0,1:T(8,128)(2,1)S(1)}, bf16[1,16,32,256]{3,2,0,1:T(8,128)(2,1)S(1)}, u32[]{:S(2)}, u32[]{:S(2)}) collective-permute-start(bf16[1,16,32,256]{3,2,0,1:T(8,128)(2,1)S(1)} %fusion.58), channel_id=1, source_target_pairs={{0,16},{16,0},{1,17},{17,1},{2,18},{18,2},{3,19},{19,3},{4,20},{20... | collective-permute-start | bytes 786440 | tf_op jit(solution)/shard_map/ppermute | solution.py:61
  65.5 16.0 %all-to-all-start.1 = ((bf16[1,16,32,256]{3,2,0,1:T(8,128)(2,1)}), bf16[1,16,32,256]{3,2,0,1:T(8,128)(2,1)S(1)}, u32[]{:S(2)}, u32[]{:S(2)}) async-start(bf16[1,16,32,256]{3,2,0,1:T(8,128)(2,1)} %fusion.55), calls=%async_computation.1 | async-start | bytes 524288 | tf_op jit(solution)/shard_map/all_to_all | solution.py:67
  71.4 10.2 %copy-start.3 = (f32[16,32,256]{2,1,0:T(8,128)S(1)}, f32[16,32,256]{2,1,0:T(8,128)}, u32[]{:S(2)}) copy-start(f32[16,32,256]{2,1,0:T(8,128)} %param.9) | copy-start | bytes 1572868
  71.4 10.2 %copy-start.4 = (f32[16,32,256]{2,1,0:T(8,128)S(1)}, f32[16,32,256]{2,1,0:T(8,128)}, u32[]{:S(2)}) copy-start(f32[16,32,256]{2,1,0:T(8,128)} %param.7) | copy-start | bytes 1572868
where the time goes:
time: 84.5 us; the launch traced here: 83.9 us
  waiting for transfers between devices  34.9 us (41%)
  matrix products  15.6 us (18%)
  starting transfers between devices  14.3 us (17%)
  other arithmetic  10.5 us (12%)
  local copies, waits for them, and re-layouts  6.24 us (7%)
  between operations  2.27 us (3%)
    all_to_all x1, waiting for transfers between devices, body(): lax.all_to_all(stacked, 'shard', split_axis=0, concat_axis=0, tiled=True)  24.4 us
    dot_general x10, matrix products, newton_schulz(): product = jnp.dot(current, poly, preferred_element_type=jnp.float32)  12.2 us
    all_to_all x1, waiting for transfers between devices, body(): lax.all_to_all(summed.astype(jnp.bfloat16), 'shard', split_axis=1, concat...  8.93 us
    all_to_all x1, starting transfers between devices, body(): lax.all_to_all(stacked, 'shard', split_axis=0, concat_axis=0, tiled=True)  8.39 us
    all_to_all x1, starting transfers between devices, body(): lax.all_to_all(summed.astype(jnp.bfloat16), 'shard', split_axis=1, concat...  5.86 us
    unnamed x20, local copies, waits for them, and re-layouts  3.88 us
    dot_general x10, matrix products, newton_schulz(): jnp.einsum('di,dj->ij', current, current, preferred_element_type=jnp.floa...  3.45 us
    add x1, other arithmetic, body(): new_shadow = shadow_decay * shadow + (1.0 - shadow_decay) * new_params  2.35 us
  transfers between devices with their start and end apart: 3, of which 3 were waited for; matrix products, arithmetic and copies ran while one was open for 1% of the time, Pallas kernels for 0%

commit v1 on v0

--- a/solution.py
+++ b/solution.py
@@ -64,9 +64,10 @@
             [(i, (i + step) % replicas) for i in range(replicas)],
         )
         summed = summed + got.astype(jnp.float32)
-    placed = lax.all_to_all(
-        summed.astype(jnp.bfloat16), "shard", split_axis=1, concat_axis=0, tiled=True
-    )
+    x = summed.astype(jnp.bfloat16)
+    pieces = jnp.split(x, lax.axis_size("shard"), axis=1)
+    arrived = lax.all_to_all(jnp.stack(pieces), "shard", 0, 0)
+    placed = jnp.concatenate(arrived, axis=0)
     outer_delta = placed.reshape((mats, rows_each, width)).astype(jnp.float32) / replicas
     new_outer = outer_mu * outer_moment + outer_delta
     new_params = params - outer_rate * (outer_delta + outer_mu * new_outer)

time: 84.5 us -> 93.5 us (1.11)
  local copies, waits for them, and re-layouts: 6.24 us -> 15.9 us
    unnamed x20 -> x35, local copies, waits for them, and re-layouts: 3.88 us -> 13 us
where the time goes in v1:
time: 93.5 us; the launch traced here: 92.9 us
  waiting for transfers between devices  34.9 us (37%)
  local copies, waits for them, and re-layouts  15.9 us (17%)
  matrix products  15.6 us (17%)
  starting transfers between devices  14.3 us (15%)
  other arithmetic  9.84 us (11%)
  between operations  2.29 us (2%)
    all_to_all x1, waiting for transfers between devices, body(): lax.all_to_all(stacked, 'shard', split_axis=0, concat_axis=0, tiled=True)  24.4 us
    unnamed x35, local copies, waits for them, and re-layouts  13 us
    dot_general x10, matrix products, newton_schulz(): product = jnp.dot(current, poly, preferred_element_type=jnp.float32)  12.2 us
    all_to_all x1, waiting for transfers between devices, body(): arrived = lax.all_to_all(jnp.stack(pieces), 'shard', 0, 0)  8.93 us
    all_to_all x1, starting transfers between devices, body(): lax.all_to_all(stacked, 'shard', split_axis=0, concat_axis=0, tiled=True)  8.39 us
    all_to_all x1, starting transfers between devices, body(): arrived = lax.all_to_all(jnp.stack(pieces), 'shard', 0, 0)  5.86 us
    dot_general x10, matrix products, newton_schulz(): jnp.einsum('di,dj->ij', current, current, preferred_element_type=jnp.floa...  3.45 us
    add x1, other arithmetic, body(): new_shadow = shadow_decay * shadow + (1.0 - shadow_decay) * new_params  2.35 us
  transfers between devices with their start and end apart: 3, of which 3 were waited for; matrix products, arithmetic and copies ran while one was open for 1% of the time, Pallas kernels for 0%

profile of v1, /device:TPU:0, one launch (start us, length us, event | category | flops | bytes accessed | tf_op | source)
XLA Modules:
  0.0 92.9 jit_solution(14557349139552856981)
XLA Ops:
  0.7 2.0 %fusion.51 = bf16[16,1,64,256]{3,2,1,0:T(8,128)(2,1)S(1)} fusion(f32[1,16,64,256]{3,2,1,0:T(8,128)} %param.6, bf16[1,2,16,64,256]{4,3,2,1,0:T(8,128)(2,1)} %param.5), kind=kLoop, calls=%fused_computation.89 | loop fusion | flops 2359296 | bytes 2621440 | tf_op jit(solution)/shard_map/convert_element_type | solution.py:44
  3.0 1.1 %pad_maximum_fusion = bf16[16,2,64,256]{3,2,1,0:T(8,128)(2,1)} fusion(bf16[16,1,64,256]{3,2,1,0:T(8,128)(2,1)S(1)} %fusion.51, bf16[16,1,64,256]{3,2,1,0:T(8,128)(2,1)S(1)} %fusion.52), kind=kLoop, calls=%fused_computation.90 | loop fusion | flops 524288 | bytes 2097152 | tf_op jit(solution)/shard_map/stack | solution.py:45
  4.1 8.4 %all-to-all-start = ((bf16[16,2,64,256]{3,2,1,0:T(8,128)(2,1)}), bf16[16,2,64,256]{3,2,1,0:T(8,128)(2,1)}, u32[]{:S(2)}, u32[]{:S(2)}) async-start(bf16[16,2,64,256]{3,2,1,0:T(8,128)(2,1)} %pad_maximum_fusion), calls=%async_computation | async-start | bytes 2097152 | tf_op jit(solution)/shard_map/all_to_all | solution.py:46
  12.5 24.4 %all-to-all-done = bf16[16,2,64,256]{3,2,1,0:T(8,128)(2,1)} async-done(((bf16[16,2,64,256]{3,2,1,0:T(8,128)(2,1)}), bf16[16,2,64,256]{3,2,1,0:T(8,128)(2,1)}, u32[]{:S(2)}, u32[]{:S(2)}) %all-to-all-start) | async-done | bytes 1048608 | tf_op jit(solution)/shard_map/all_to_all | solution.py:46
  36.9 1.3 %copy.32 = bf16[16,2,64,256]{3,2,0,1:T(8,128)(2,1)S(1)} copy(bf16[16,2,64,256]{3,2,1,0:T(8,128)(2,1)} %all-to-all-done) | data formatting | bytes 2097152 | tf_op jit(solution)/shard_map/all_to_all | solution.py:46
  38.2 0.9 fusion.40
  40.5 1.0 %fusion.41 = (bf16[16,1,1,64,256]{4,3,0,2,1:T(8,128)(2,1)S(1)}, bf16[16,1,1,64,256]{4,3,0,2,1:T(8,128)(2,1)}) fusion(f32[]{:T(128)S(6)} %add.149, bf16[16,1,2,64,256]{4,3,0,2,1:T(8,128)(2,1)S(1)} %bitcast.216, f32[]{:T(128)S(6)} %add.160), kind=kLoop, calls=%fused_computation.79 | loop fusion | flops 1572864 | bytes 2097160 | tf_op jit(solution)/shard_map/convert_element_type | solution.py:19
  42.3 1.7 %fusion.4 = bf16[1024,256]{1,0:T(8,128)(2,1)S(1)} fusion(bf16[1024,256]{1,0:T(8,128)(2,1)} %bitcast.220, bf16[256,256]{1,0:T(8,128)(2,1)S(1)} %fusion.28), kind=kOutput, calls=%fused_computation.22 | convolution fusion | flops 169148416 | bytes 1179648 | tf_op jit(solution)/shard_map/dot_general | solution.py:26
  45.8 0.8 copy-done.8
  46.9 1.7 %fusion.7 = bf16[1024,256]{1,0:T(8,128)(2,1)S(1)} fusion(bf16[1024,256]{1,0:T(8,128)(2,1)} %copy-done.8, bf16[256,256]{1,0:T(8,128)(2,1)S(1)} %convolution_convert_fusion.5), kind=kOutput, calls=%fused_computation.25 | convolution fusion | flops 169148416 | bytes 1179648 | tf_op jit(solution)/shard_map/dot_general | solution.py:26
  52.6 0.8 copy-done.9
  53.7 1.7 %fusion.15 = bf16[1024,256]{1,0:T(8,128)(2,1)S(1)} fusion(bf16[1024,256]{1,0:T(8,128)(2,1)} %copy-done.9, bf16[256,256]{1,0:T(8,128)(2,1)S(1)} %convolution_convert_fusion.1), kind=kOutput, calls=%fused_computation.33 | convolution fusion | flops 169148416 | bytes 1179648 | tf_op jit(solution)/shard_map/dot_general | solution.py:26
  55.4 0.8 copy-done.2
  56.6 1.7 %fusion.17 = f32[1024,256]{1,0:T(8,128)S(1)} fusion(bf16[1024,256]{1,0:T(8,128)(2,1)} %copy-done.2, bf16[256,256]{1,0:T(8,128)(2,1)S(1)} %convolution_convert_fusion), kind=kOutput, calls=%fused_computation.35 | convolution fusion | flops 169410560 | bytes 1703936 | tf_op jit(solution)/shard_map/dot_general | solution.py:26
  58.3 2.7 %fusion.11 = f32[1024,256]{1,0:T(8,128)} fusion(f32[1024,256]{1,0:T(8,128)S(1)} %fusion.17, bf16[1024,256]{1,0:T(8,128)(2,1)} %copy-done.5, bf16[256,256]{1,0:T(8,128)(2,1)S(1)} %convolution_convert_fusion.4), kind=kOutput, calls=%fused_computation.29 | convolution fusion | flops 169934848 | bytes 2752512 | tf_op jit(solution)/shard_map/dot_general | solution.py:26
  61.0 1.1 %fusion.58 = bf16[1,16,32,256]{3,2,1,0:T(8,128)(2,1)S(1)} fusion(f32[1,16,2,32,256]{4,3,2,1,0:T(8,128)} %bitcast.217, s32[]{:T(128)S(6)} %select_n.16), kind=kLoop, calls=%fused_computation.104 | loop fusion | bytes 524292 | tf_op jit(solution)/shard_map/convert_element_type | solution.py:62
  62.1 1.5 %collective-permute-done = bf16[1,16,32,256]{3,2,1,0:T(8,128)(2,1)S(1)} collective-permute-done((bf16[1,16,32,256]{3,2,1,0:T(8,128)(2,1)S(1)}, bf16[1,16,32,256]{3,2,1,0:T(8,128)(2,1)S(1)}, u32[]{:S(2)}, u32[]{:S(2)}) %collective-permute-start) | collective-permute-done | bytes 262176 | tf_op jit(solution)/shard_map/ppermute | solution.py:61
  63.7 1.1 %fusion.55 = bf16[1,16,32,256]{3,2,1,0:T(8,128)(2,1)S(1)} fusion(bf16[1,16,32,256]{3,2,1,0:T(8,128)(2,1)S(1)} %collective-permute-done, f32[1,16,2,32,256]{4,3,2,1,0:T(8,128)} %bitcast.218, s32[]{:T(128)S(6)} %select_n.14), kind=kLoop, calls=%fused_computation.99 | loop fusion | flops 393216 | bytes 1048580 | tf_op jit(solution)/shard_map/convert_element_type | solution.py:67
  64.8 0.6 constant_dynamic-update-slice_fusion.15
  65.4 0.6 constant_dynamic-update-slice_fusion.14
  66.0 0.6 constant_dynamic-update-slice_fusion.13
  66.6 0.6 constant_dynamic-update-slice_fusion.12
  67.2 0.6 constant_dynamic-update-slice_fusion.11
  67.8 0.6 constant_dynamic-update-slice_fusion.10
  68.4 0.6 constant_dynamic-update-slice_fusion.9
  70.3 0.6 constant_dynamic-update-slice_fusion.6
  70.9 0.6 constant_dynamic-update-slice_fusion.5
  71.5 0.6 constant_dynamic-update-slice_fusion.4
  74.5 5.9 %all-to-all-start.1 = ((bf16[16,1,1,32,256]{4,3,2,1,0:T(8,128)(2,1)}), bf16[16,1,1,32,256]{4,3,2,1,0:T(8,128)(2,1)S(1)}, u32[]{:S(2)}, u32[]{:S(2)}) async-start(bf16[16,1,1,32,256]{4,3,2,1,0:T(8,128)(2,1)} %constant_dynamic-update-slice_fusion), calls=%async_computation.1 | async-start | bytes 524288 | tf_op jit(solution)/shard_map/all_to_all | solution.py:69
  80.4 1.2 %fusion.49 = f32[1,16,64,256]{3,2,1,0:T(8,128)} fusion(f32[1,16,64,256]{3,2,1,0:T(8,128)S(1)} %copy-done, bf16[1,2,16,64,256]{4,3,2,1,0:T(8,128)(2,1)S(1)} %copy-done.1), kind=kLoop, calls=%fused_computation.87 | loop fusion | flops 1572864 | bytes 3145728 | tf_op jit(solution)/shard_map/add | solution.py:43
  81.6 8.9 %all-to-all-done.1 = bf16[16,1,1,32,256]{4,3,2,1,0:T(8,128)(2,1)S(1)} async-done(((bf16[16,1,1,32,256]{4,3,2,1,0:T(8,128)(2,1)}), bf16[16,1,1,32,256]{4,3,2,1,0:T(8,128)(2,1)S(1)}, u32[]{:S(2)}, u32[]{:S(2)}) %all-to-all-start.1) | async-done | bytes 262176 | tf_op jit(solution)/shard_map/all_to_all | solution.py:69
  90.5 2.4 %multiply_add_fusion = (f32[16,32,256]{2,1,0:T(8,128)}, f32[16,32,256]{2,1,0:T(8,128)}, f32[16,32,256]{2,1,0:T(8,128)}) fusion(f32[16,32,256]{2,1,0:T(8,128)S(1)} %copy-done.3, f32[16,32,256]{2,1,0:T(8,128)S(1)} %copy-done.4, bf16[16,1,1,32,256]{4,3,2,1,0:T(8,128)(2,1)S(1)} %all-to-all-done.1, f32[16,32,256]{2,1,0:T(8,128)} %param.8), kind=kLoop, calls=%fused_computation.102 | loop fusion | flops 1441792 | bytes 3407872 | tf_op jit(solution)/shard_map/add | solution.py:74
  (40 shorter events, 11.5 us)
Async XLA Ops:
  0.6 2.0 %copy-start.1 = (bf16[1,2,16,64,256]{4,3,2,1,0:T(8,128)(2,1)S(1)}, bf16[1,2,16,64,256]{4,3,2,1,0:T(8,128)(2,1)}, u32[]{:S(2)}) copy-start(bf16[1,2,16,64,256]{4,3,2,1,0:T(8,128)(2,1)} %param.5) | copy-start | bytes 3145732
  0.6 2.2 %copy-start = (f32[1,16,64,256]{3,2,1,0:T(8,128)S(1)}, f32[1,16,64,256]{3,2,1,0:T(8,128)}, u32[]{:S(2)}) copy-start(f32[1,16,64,256]{3,2,1,0:T(8,128)} %param.6) | copy-start | bytes 3145732
  4.1 32.8 %all-to-all-start = ((bf16[16,2,64,256]{3,2,1,0:T(8,128)(2,1)}), bf16[16,2,64,256]{3,2,1,0:T(8,128)(2,1)}, u32[]{:S(2)}, u32[]{:S(2)}) async-start(bf16[16,2,64,256]{3,2,1,0:T(8,128)(2,1)} %pad_maximum_fusion), calls=%async_computation | async-start | bytes 2097152 | tf_op jit(solution)/shard_map/all_to_all | solution.py:46
  41.5 0.8 copy-start.7
  45.8 0.8 copy-start.8
  48.7 0.8 copy-start.5
  48.7 1.2 %copy-start.6 = (bf16[16,1,1,64,256]{4,3,0,2,1:T(8,128)(2,1)S(1)}, bf16[16,1,1,64,256]{4,3,0,2,1:T(8,128)(2,1)}, u32[]{:S(2)}) copy-start(bf16[16,1,1,64,256]{4,3,0,2,1:T(8,128)(2,1)} %get-tuple-element.10) | copy-start | bytes 1572868
  52.5 0.8 copy-start.9
  55.4 0.8 copy-start.2
  62.1 1.6 %collective-permute-start = (bf16[1,16,32,256]{3,2,1,0:T(8,128)(2,1)S(1)}, bf16[1,16,32,256]{3,2,1,0:T(8,128)(2,1)S(1)}, u32[]{:S(2)}, u32[]{:S(2)}) collective-permute-start(bf16[1,16,32,256]{3,2,1,0:T(8,128)(2,1)S(1)} %fusion.58), channel_id=1, source_target_pairs={{0,16},{16,0},{1,17},{17,1},{2,18},{18,2},{3,19},{19,3},{4,20},{20... | collective-permute-start | bytes 786440 | tf_op jit(solution)/shard_map/ppermute | solution.py:61
  74.5 16.0 %all-to-all-start.1 = ((bf16[16,1,1,32,256]{4,3,2,1,0:T(8,128)(2,1)}), bf16[16,1,1,32,256]{4,3,2,1,0:T(8,128)(2,1)S(1)}, u32[]{:S(2)}, u32[]{:S(2)}) async-start(bf16[16,1,1,32,256]{4,3,2,1,0:T(8,128)(2,1)} %constant_dynamic-update-slice_fusion), calls=%async_computation.1 | async-start | bytes 524288 | tf_op jit(solution)/shard_map/all_to_all | solution.py:69
  80.4 10.2 %copy-start.3 = (f32[16,32,256]{2,1,0:T(8,128)S(1)}, f32[16,32,256]{2,1,0:T(8,128)}, u32[]{:S(2)}) copy-start(f32[16,32,256]{2,1,0:T(8,128)} %param.9) | copy-start | bytes 1572868
  80.4 10.2 %copy-start.4 = (f32[16,32,256]{2,1,0:T(8,128)S(1)}, f32[16,32,256]{2,1,0:T(8,128)}, u32[]{:S(2)}) copy-start(f32[16,32,256]{2,1,0:T(8,128)} %param.7) | copy-start | bytes 1572868
